TPU v7x, 256 devices: a whole 4x4x8 slice. The times are simulated.
256 devices in a mesh: seq: 32 (over z_hi, x, core), head: 8 (over y, z_lo).
Axes of the slice: x: 4, y: 4, z: 8 (z_hi: 4, z_lo: 2; z = z_hi * 2 + z_lo), core: 2. Of those that a mesh axis runs over, the one named last changes fastest.
Arguments:
- queries: bfloat16 [6144, 4096], P('seq', 'head'), may hold values from -12.5 to 12.5
- keys: bfloat16 [6144, 1024], P('seq', 'head'), may hold values from -10.5 to 10.5
- values: bfloat16 [6144, 1024], P('seq', 'head'), may hold values from -6 to 6
- d_out: bfloat16 [6144, 4096], P('seq', 'head'), may hold values from -6 to 6
- w_out: bfloat16 [4096, 4096], P('head'), may hold values from -0.09375 to 0.09375
- doc_starts: int32 [4], replicated, may hold values from 0 to 6128, as said below
Outputs:
- query_grad: bfloat16 [6144, 4096], P('seq', 'head')
- key_grad: bfloat16 [6144, 1024], P('seq', 'head')
- value_grad: bfloat16 [6144, 1024], P('seq', 'head')
Inputs may be any that keep to these rules, and one draw needn't show every extreme that they name: doc_starts[0] is 0, the entries rise strictly, every entry is a multiple of 16, and the last entry is 6128, so the last document has 16 positions; a document runs from its start to the next start or to the end of the sequence.
All inputs are finite; a program needn't handle non-finite values.
Results may differ from a plain program's by a relative error of at most 0.0163.
Values may be sent and summed in bfloat16 or wider, within the bound.
A program may use at most 128 MiB of HBM per device.

v0:
```python
import math
import jax
import jax.numpy as jnp
from jax import lax
from jax.sharding import PartitionSpec as P

DH = 128
NEG_FILL = -1e30


def doc_index(doc_starts, places):
    return jnp.sum((places[:, None] >= doc_starts[None, :]).astype(jnp.int32), axis=1)


def allowed_pairs(doc_starts, row_ids, col_ids):
    earlier = col_ids[None, :] <= row_ids[:, None]
    same_doc = doc_index(doc_starts, row_ids)[:, None] == doc_index(doc_starts, col_ids)[None, :]
    return (earlier & same_doc)[None, None]


def softmax_grads(q_four, g_four, key_three, value_three, allowed, log_total, row_delta, scaling):
    scores = (
        jnp.einsum("sghd,kgd->ghsk", q_four, key_three, preferred_element_type=jnp.float32)
        * scaling
    )
    prob_full = jnp.where(allowed, jnp.exp(scores - log_total[..., None]), 0.0)
    grad_dots = jnp.einsum(
        "sghd,kgd->ghsk", g_four, value_three, preferred_element_type=jnp.float32
    )
    dscores = prob_full * (grad_dots - row_delta[..., None]) * scaling
    return (prob_full.astype(jnp.bfloat16), dscores.astype(jnp.bfloat16))


def shards(queries, keys, values, d_out, w_out, doc_starts):
    rows_here = queries.shape[0]
    head_size = DH
    groups = keys.shape[1] // head_size
    per_group = queries.shape[1] // keys.shape[1]
    scaling = 1.0 / math.sqrt(head_size)
    first_row = lax.axis_index("seq") * rows_here
    my_rows = first_row + jnp.arange(rows_here, dtype=jnp.int32)
    weights = w_out
    attn_grad = lax.dot_general(
        lax.all_gather(d_out, "head", axis=1, tiled=True),
        weights,
        (((1,), (1,)), ((), ())),
        preferred_element_type=jnp.float32,
    )
    attn_grad = attn_grad.astype(jnp.bfloat16)
    query_four = queries.reshape(rows_here, groups, per_group, head_size)
    grad_four = attn_grad.reshape(rows_here, groups, per_group, head_size)
    stat_shape = (groups, per_group, rows_here)
    key_block = lax.all_gather(keys, "seq", axis=0, tiled=True)
    value_block = lax.all_gather(values, "seq", axis=0, tiled=True)
    piece_rows = key_block.shape[0]
    allowed = allowed_pairs(doc_starts, my_rows, jnp.arange(piece_rows, dtype=jnp.int32))
    key_three = key_block.reshape(piece_rows, groups, head_size)
    value_three = value_block.reshape(piece_rows, groups, head_size)
    scores = (
        jnp.einsum("sghd,kgd->ghsk", query_four, key_three, preferred_element_type=jnp.float32)
        * scaling
    )
    scores = jnp.where(allowed, scores, NEG_FILL)
    high_old = jnp.full(stat_shape, NEG_FILL, jnp.float32)
    high_new = jnp.maximum(high_old, jnp.max(scores, axis=-1))
    weights = jnp.where(allowed, jnp.exp(scores - high_new[..., None]), 0.0)
    grad_dots = jnp.einsum(
        "sghd,kgd->ghsk", grad_four, value_three, preferred_element_type=jnp.float32
    )
    total_new = jnp.sum(weights, axis=-1)
    accum_new = jnp.sum(weights * grad_dots, axis=-1)
    log_total = high_new + jnp.log(total_new)
    row_delta = accum_new / total_new
    key_block = lax.all_gather(keys, "seq", axis=0, tiled=True)
    value_block = lax.all_gather(values, "seq", axis=0, tiled=True)
    piece_rows = key_block.shape[0]
    allowed = allowed_pairs(doc_starts, my_rows, jnp.arange(piece_rows, dtype=jnp.int32))
    key_three = key_block.reshape(piece_rows, groups, head_size)
    value_three = value_block.reshape(piece_rows, groups, head_size)
    prob_half, dscores = softmax_grads(
        query_four, grad_four, key_three, value_three, allowed, log_total, row_delta, scaling
    )
    key_three, prob_half, dscores, piece_rows = (key_three, prob_half, dscores, piece_rows)
    query_acc = jnp.einsum("ghsk,kgd->sghd", dscores, key_three, preferred_element_type=jnp.float32)
    key_piece = jnp.einsum(
        "ghsk,sghd->kgd", dscores, query_four, preferred_element_type=jnp.float32
    )
    value_piece = jnp.einsum(
        "ghsk,sghd->kgd", prob_half, grad_four, preferred_element_type=jnp.float32
    )
    key_acc = key_piece
    value_acc = value_piece
    query_acc, key_terms, value_terms = (query_acc, key_acc, value_acc)
    key_acc, value_acc = (
        lax.psum_scatter(
            key_terms.astype(jnp.bfloat16), "seq", scatter_dimension=0, tiled=True
        ).astype(jnp.float32),
        lax.psum_scatter(
            value_terms.astype(jnp.bfloat16), "seq", scatter_dimension=0, tiled=True
        ).astype(jnp.float32),
    )
    query_grad = query_acc.reshape(rows_here, groups * per_group * head_size).astype(jnp.bfloat16)
    key_grad = key_acc.reshape(rows_here, groups * head_size).astype(jnp.bfloat16)
    value_grad = value_acc.reshape(rows_here, groups * head_size).astype(jnp.bfloat16)
    return (query_grad, key_grad, value_grad)


def solution(mesh):
    return jax.shard_map(
        shards,
        mesh=mesh,
        in_specs=(
            P("seq", "head"),
            P("seq", "head"),
            P("seq", "head"),
            P("seq", "head"),
            P("head", None),
            P(),
        ),
        out_specs=(P("seq", "head"), P("seq", "head"), P("seq", "head")),
        check_vma=False,
    )
```

profile of v0, /device:TPU:8, one launch (start us, length us, event | category | flops | bytes accessed | tf_op | source)
XLA Modules:
  0.0 378.5 jit_solution(6322208966597983329)
XLA Ops:
  7.2 0.0 copy-start
  7.2 0.0 all-gather.6.cloned.1.call-start
  7.2 0.7 all-gather.6.cloned.1.call-update
  7.9 0.0 all-gather.4.cloned.1.call-start
  8.0 0.7 all-gather.4.cloned.1.call-update
  8.7 0.0 all-gather.8.cloned.1.call-start
  8.7 0.7 all-gather.8.cloned.1.call-update
  9.4 0.0 reduce-scatter.7.cloned.1.call-start
  9.5 0.7 convert_reduce_fusion.1
  10.2 0.8 convert_reduce_fusion
  11.0 1.0 fusion.25
  12.0 45.0 %all-gather.6.cloned.1.call-done = bf16[192,4096]{1,0:T(8,128)(2,1)} async-done(((bf16[192,512]{1,0:T(8,128)(2,1)}), bf16[192,4096]{1,0:T(8,128)(2,1)}) %all-gather.6.cloned.1.call-update) | async-done | bytes 1572880 | tf_op jit(solution)/shard_map/all_gather | solution.py:44
  57.0 4.2 %fusion.38 = bf16[24,4,8,128]{3,2,1,0:T(8,128)(2,1)S(1)} fusion(bf16[192,4096]{1,0:T(8,128)(2,1)} %all-gather.6.cloned.1.call-done, bf16[512,4096]{1,0:T(8,128)(2,1)} %param.10), kind=kOutput, calls=%fused_computation.35 | convolution fusion | flops 805404672 | bytes 5963776 | tf_op jit(solution)/shard_map/dot_general | solution.py:43
  61.2 52.1 %all-gather.4.cloned.1.call-done = bf16[6144,128]{1,0:T(8,128)(2,1)} async-done(((bf16[192,128]{1,0:T(8,128)(2,1)}), bf16[6144,128]{1,0:T(8,128)(2,1)}) %all-gather.4.cloned.1.call-update) | async-done | bytes 1572880 | tf_op jit(solution)/shard_map/all_gather | solution.py:74
  113.3 0.0 copy-done
  113.3 9.9 %fusion.6 = (f32[4,192]{1,0:T(4,128)S(1)}, f32[6144,192,4]{0,1,2:T(8,128)}) fusion(pred[192,6144]{1,0:T(8,128)(4,1)S(1)} %fusion.25, bf16[6144,128]{1,0:T(8,128)(2,1)} %all-gather.4.cloned.1.call-done, bf16[192,512]{1,0:T(8,128)(2,1)S(1)} %copy-done), kind=kOutput, calls=%fused_computation.11 | convolution fusion | flops 1222114560 | bytes 21826560 | tf_op jit(solution)/shard_map/sghd,kgd->ghsk/dot_general | solution.py:23
  123.2 43.0 %all-gather.8.cloned.1.call-done = bf16[6144,128]{1,0:T(8,128)(2,1)} async-done(((bf16[192,128]{1,0:T(8,128)(2,1)}), bf16[6144,128]{1,0:T(8,128)(2,1)}) %all-gather.8.cloned.1.call-update) | async-done | bytes 1572880 | tf_op jit(solution)/shard_map/all_gather | solution.py:75
  166.2 15.5 %fusion.8 = (f32[4,192]{1,0:T(4,128)S(1)}, f32[4,192]{1,0:T(4,128)S(1)}, f32[192,4,6144]{2,0,1:T(8,128)}) fusion(f32[6144,192,4]{0,1,2:T(8,128)} %get-tuple-element.20, f32[4,192]{1,0:T(4,128)S(1)} %broadcast_maximum_fusion, pred[192,6144]{1,0:T(8,128)(4,1)S(1)} %fusion.25, bf16[6144,128]{1,0:T(8,128)(2,1)} %all-gather.8.cloned.1.call-done, ...), kind=kOutput, calls=%fused_computation.13 | convolution fusion | flops 1240988160 | bytes 40707072 | tf_op jit(solution)/shard_map/sghd,kgd->ghsk/dot_general | solution.py:27
  181.8 9.1 %fusion.21 = bf16[6144,128]{0,1:T(8,128)(2,1)S(1)} fusion(f32[6144,192,4]{0,1,2:T(8,128)} %get-tuple-element.20, f32[4,192]{1,0:T(4,128)S(1)} %get-tuple-element.17, pred[192,6144]{1,0:T(8,128)(4,1)S(1)} %fusion.25, bf16[24,4,8,128]{3,2,1,0:T(8,128)(2,1)S(1)} %fusion.38), kind=kOutput, calls=%fused_computation.22 | convolution fusion | flops 1227620352 | bytes 21826560 | tf_op jit(solution)/shard_map/ghsk,sghd->kgd/dot_general | solution.py:88
  190.8 1.6 copy.34
  192.4 0.0 reduce-scatter.7.cloned.1.call-update
  192.5 0.2 reduce-scatter.5.cloned.1.call-start
  192.7 13.7 %fusion.10 = bf16[4,192,6144]{2,1,0:T(8,128)(2,1)S(1)} fusion(f32[192,4,6144]{2,0,1:T(8,128)} %get-tuple-element.21, f32[6144,192,4]{0,1,2:T(8,128)} %get-tuple-element.20, f32[4,192]{1,0:T(4,128)S(1)} %get-tuple-element.18, f32[4,192]{1,0:T(4,128)S(1)} %get-tuple-element.17, pred[192,6144]{1,0:T(8,128)(4,1)S(1)} %fusion.25), kind=kLoop, calls=%fused_computation.15 | loop fusion | flops 33030144 | bytes 48371712 | tf_op jit(solution)/shard_map/reshape.24
  206.4 0.0 copy-start.1
  206.4 3.6 copy-done.1
  210.0 0.0 copy-start.2
  210.0 3.9 %fusion.24 = bf16[6144,1,128]{2,0,1:T(8,128)(2,1)} fusion(bf16[4,192,6144]{2,1,0:T(8,128)(2,1)S(1)} %fusion.10, bf16[192,512]{1,0:T(8,128)(2,1)S(1)} %copy-done), kind=kOutput, calls=%fused_computation.23 | convolution fusion | flops 1208745984 | bytes 11206656 | tf_op jit(solution)/shard_map/ghsk,sghd->kgd/dot_general | solution.py:85
  213.9 0.0 reduce-scatter.5.cloned.1.call-update
  213.9 0.0 copy-done.2
  213.9 6.4 %fusion.35 = bf16[192,1,4,128]{3,0,2,1:T(8,128)(2,1)S(1)} fusion(bf16[4,192,6144]{2,1,0:T(8,128)(2,1)} %copy-done.1, bf16[6144,128]{1,0:T(8,128)(2,1)S(1)} %copy-done.2), kind=kOutput, calls=%fused_computation.34 | convolution fusion | flops 1208057856 | bytes 11206656 | tf_op jit(solution)/shard_map/ghsk,kgd->sghd/dot_general | solution.py:84
  220.3 0.2 copy.28
  220.5 0.7 copy.60
  221.2 58.7 %reduce-scatter.7.cloned.1.call-done = bf16[192,128]{1,0:T(8,128)(2,1)} async-done(((bf16[6144,128]{1,0:T(8,128)(2,1)}), bf16[192,128]{1,0:T(8,128)(2,1)}) %reduce-scatter.7.cloned.1.call-update) | async-done | bytes 49168
  279.9 92.1 %reduce-scatter.5.cloned.1.call-done = bf16[192,1,128]{2,0,1:T(8,128)(2,1)} async-done(((bf16[6144,1,128]{2,0,1:T(8,128)(2,1)}), bf16[192,1,128]{2,0,1:T(8,128)(2,1)}) %reduce-scatter.5.cloned.1.call-update) | async-done | bytes 49168 | tf_op jit(solution)/shard_map/reduce_scatter | solution.py:95
  (3 shorter events, 0.0 us)
Async XLA Ops:
  7.2 106.2 %copy-start = (bf16[192,512]{1,0:T(8,128)(2,1)S(1)}, bf16[192,512]{1,0:T(8,128)(2,1)}, u32[]{:S(2)}) copy-start(bf16[192,512]{1,0:T(8,128)(2,1)} %param.6) | copy-start | bytes 589828
  7.2 49.8 %all-gather.6.cloned.1.call-start = ((), (), s32[]{:S(2)}) async-start(), calls=%async_computation.3 | async-start | bytes 1769472 | tf_op jit(solution)/shard_map/all_gather | solution.py:44
  7.9 105.4 %all-gather.4.cloned.1.call-start = ((), (), s32[]{:S(2)}) async-start(), calls=%async_computation.2 | async-start | bytes 1622016 | tf_op jit(solution)/shard_map/all_gather | solution.py:74
  8.7 157.5 %all-gather.8.cloned.1.call-start = ((), (), s32[]{:S(2)}) async-start(), calls=%async_computation.4 | async-start | bytes 1622016 | tf_op jit(solution)/shard_map/all_gather | solution.py:75
  9.4 270.5 %reduce-scatter.7.cloned.1.call-start = ((), (), s32[]{:S(2)}) async-start(), calls=%async_computation.6 | async-start | bytes 1622016
  192.5 179.5 %reduce-scatter.5.cloned.1.call-start = ((), (), s32[]{:S(2)}) async-start(), calls=%async_computation.5 | async-start | bytes 1622016 | tf_op jit(solution)/shard_map/reduce_scatter | solution.py:95
  206.4 3.6 copy-start.1
  210.0 3.9 %copy-start.2 = (bf16[6144,128]{1,0:T(8,128)(2,1)S(1)}, bf16[6144,128]{1,0:T(8,128)(2,1)}, u32[]{:S(2)}) copy-start(bf16[6144,128]{1,0:T(8,128)(2,1)} %all-gather.4.cloned.1.call-done) | copy-start | bytes 4718596
Sparse Core Ops, SparseCore 0:
  9.8 47.1 all-gather.5
  59.5 53.7 all-gather.3
  115.9 50.2 all-gather.7
  192.6 87.3 reduce-scatter.6
  284.2 87.7 reduce-scatter.4
where the time goes:
time: 379 us
  waiting for transfers between devices  293 us (77%)
  matrix products  49 us (13%)
  other arithmetic  16.2 us (4%)
  between operations  13.9 us (4%)
  local copies, waits for them, and re-layouts  6.1 us (2%)
    reduce_scatter x1, waiting for transfers between devices, shards(): lax.psum_scatter(key_terms.astype(jnp.bfloat16), 'seq', scatter_dimension...  92.1 us
    unnamed x6, waiting for transfers between devices  60.8 us
    all_gather x1, waiting for transfers between devices, shards(): key_block = lax.all_gather(keys, 'seq', axis=0, tiled=True)  52.1 us
    all_gather x1, waiting for transfers between devices, shards(): lax.all_gather(d_out, 'head', axis=1, tiled=True)  45 us
    all_gather x1, waiting for transfers between devices, shards(): value_block = lax.all_gather(values, 'seq', axis=0, tiled=True)  43 us
    dot_general x1, matrix products, softmax_grads(): jnp.einsum('sghd,kgd->ghsk', g_four, value_three, preferred_element_type=...  15.5 us
    another operation x1, other arithmetic  13.7 us
    dot_general x1, matrix products, softmax_grads(): jnp.einsum('sghd,kgd->ghsk', q_four, key_three, preferred_element_type=jn...  9.9 us
  transfers between devices with their start and end apart: 5, of which 5 were waited for; matrix products, arithmetic and copies ran while one was open for 11% of the time, Pallas kernels for 0%

commit v1 on v0

--- a/solution.py
+++ b/solution.py
@@ -41,7 +41,9 @@
     my_rows = first_row + jnp.arange(rows_here, dtype=jnp.int32)
     weights = w_out
     attn_grad = lax.dot_general(
-        lax.all_gather(d_out, "head", axis=1, tiled=True),
+        jnp.concatenate(
+            lax.all_to_all(jnp.stack([d_out] * lax.axis_size("head")), "head", 0, 0), axis=1
+        ),
         weights,
         (((1,), (1,)), ((), ())),
         preferred_element_type=jnp.float32,

time: 379 us -> 332 us (0.88)
  waiting for transfers between devices: 293 us -> 238 us
  starting transfers between devices: 0.37 us -> 6.57 us
    all_gather x1 -> x0, waiting for transfers between devices: 45 us -> none  [shards(): lax.all_gather(d_out, 'head', axis=1, tiled=True)]
    all_gather x1, waiting for transfers between devices: 52.1 us -> 26.4 us  [shards(): key_block = lax.all_gather(keys, 'seq', axis=0, tiled=True)]
    all_to_all x0 -> x1, waiting for transfers between devices: none -> 16.6 us  [shards(): lax.all_to_all(jnp.stack([d_out] * lax.axis_size('head')), 'head', 0, 0)]
    all_to_all x0 -> x1, starting transfers between devices: none -> 6.27 us  [shards(): lax.all_to_all(jnp.stack([d_out] * lax.axis_size('head')), 'head', 0, 0)]
    unnamed x6 -> x5, waiting for transfers between devices: 60.8 us -> 60.2 us
  transfers between devices with their start and end apart: 5 -> 5, of which waited for: 5 -> 5; matrix products, arithmetic and copies ran while one was open for 11% -> 13% of each run, Pallas kernels for 0% -> 0%
where the time goes in v1:
time: 332 us
  waiting for transfers between devices  238 us (72%)
  matrix products  48.6 us (15%)
  other arithmetic  16.2 us (5%)
  between operations  13.8 us (4%)
  local copies, waits for them, and re-layouts  8.46 us (3%)
  starting transfers between devices  6.57 us (2%)
    reduce_scatter x1, waiting for transfers between devices, shards(): lax.psum_scatter(key_terms.astype(jnp.bfloat16), 'seq', scatter_dimension...  92.1 us
    unnamed x5, waiting for transfers between devices  60.2 us
    all_gather x1, waiting for transfers between devices, shards(): value_block = lax.all_gather(values, 'seq', axis=0, tiled=True)  43 us
    all_gather x1, waiting for transfers between devices, shards(): key_block = lax.all_gather(keys, 'seq', axis=0, tiled=True)  26.4 us
    all_to_all x1, waiting for transfers between devices, shards(): lax.all_to_all(jnp.stack([d_out] * lax.axis_size('head')), 'head', 0, 0)  16.6 us
    dot_general x1, matrix products, softmax_grads(): jnp.einsum('sghd,kgd->ghsk', g_four, value_three, preferred_element_type=...  15.5 us
    another operation x1, other arithmetic  13.7 us
    dot_general x1, matrix products, softmax_grads(): jnp.einsum('sghd,kgd->ghsk', q_four, key_three, preferred_element_type=jn...  9.91 us
  transfers between devices with their start and end apart: 5, of which 5 were waited for; matrix products, arithmetic and copies ran while one was open for 13% of the time, Pallas kernels for 0%

profile of v1, /device:TPU:8, one launch (start us, length us, event | category | flops | bytes accessed | tf_op | source)
XLA Modules:
  0.0 332.0 jit_solution(15713102429166708088)
XLA Ops:
  7.2 0.0 copy-start
  7.2 0.0 all-gather.3.cloned.1.call-start
  7.2 0.7 all-gather.3.cloned.1.call-update
  7.9 2.2 stack.2
  10.1 6.3 %all-to-all-start = ((bf16[8,192,512]{2,1,0:T(8,128)(2,1)}), bf16[8,192,512]{2,1,0:T(8,128)(2,1)S(1)}, u32[]{:S(2)}, u32[]{:S(2)}) async-start(bf16[8,192,512]{2,1,0:T(8,128)(2,1)} %stack.2), calls=%async_computation | async-start | bytes 3145728 | tf_op jit(solution)/shard_map/all_to_all | solution.py:45
  16.4 0.0 all-gather.5.cloned.1.call-start
  16.4 0.7 all-gather.5.cloned.1.call-update
  17.1 0.0 reduce-scatter.7.cloned.1.call-start
  17.2 0.7 convert_reduce_fusion.1
  17.9 0.8 convert_reduce_fusion
  18.7 1.0 fusion.25
  19.7 16.6 %all-to-all-done = bf16[8,192,512]{2,1,0:T(8,128)(2,1)S(1)} async-done(((bf16[8,192,512]{2,1,0:T(8,128)(2,1)}), bf16[8,192,512]{2,1,0:T(8,128)(2,1)S(1)}, u32[]{:S(2)}, u32[]{:S(2)}) %all-to-all-start) | async-done | bytes 1572896 | tf_op jit(solution)/shard_map/all_to_all | solution.py:45
  36.3 0.2 copy.40
  36.5 3.8 %fusion.38 = bf16[24,4,8,128]{3,2,1,0:T(8,128)(2,1)S(1)} fusion(bf16[192,4096]{1,0:T(8,128)(2,1)S(1)} %bitcast.148, bf16[512,4096]{1,0:T(8,128)(2,1)} %param.10), kind=kOutput, calls=%fused_computation.35 | convolution fusion | flops 805404672 | bytes 5963776 | tf_op jit(solution)/shard_map/dot_general | solution.py:43
  40.4 26.4 %all-gather.3.cloned.1.call-done = bf16[6144,128]{1,0:T(8,128)(2,1)} async-done(((bf16[192,128]{1,0:T(8,128)(2,1)}), bf16[6144,128]{1,0:T(8,128)(2,1)}) %all-gather.3.cloned.1.call-update) | async-done | bytes 1572880 | tf_op jit(solution)/shard_map/all_gather | solution.py:76
  66.7 0.0 copy-done
  66.7 9.9 %fusion.6 = (f32[4,192]{1,0:T(4,128)S(1)}, f32[6144,192,4]{0,1,2:T(8,128)}) fusion(pred[192,6144]{1,0:T(8,128)(4,1)S(1)} %fusion.25, bf16[6144,128]{1,0:T(8,128)(2,1)} %all-gather.3.cloned.1.call-done, bf16[192,512]{1,0:T(8,128)(2,1)S(1)} %copy-done), kind=kOutput, calls=%fused_computation.11 | convolution fusion | flops 1222114560 | bytes 21826560 | tf_op jit(solution)/shard_map/sghd,kgd->ghsk/dot_general | solution.py:23
  76.6 43.0 %all-gather.5.cloned.1.call-done = bf16[6144,128]{1,0:T(8,128)(2,1)} async-done(((bf16[192,128]{1,0:T(8,128)(2,1)}), bf16[6144,128]{1,0:T(8,128)(2,1)}) %all-gather.5.cloned.1.call-update) | async-done | bytes 1572880 | tf_op jit(solution)/shard_map/all_gather | solution.py:77
  119.6 15.5 %fusion.8 = (f32[4,192]{1,0:T(4,128)S(1)}, f32[4,192]{1,0:T(4,128)S(1)}, f32[192,4,6144]{2,0,1:T(8,128)}) fusion(f32[6144,192,4]{0,1,2:T(8,128)} %get-tuple-element.20, f32[4,192]{1,0:T(4,128)S(1)} %broadcast_maximum_fusion, pred[192,6144]{1,0:T(8,128)(4,1)S(1)} %fusion.25, bf16[6144,128]{1,0:T(8,128)(2,1)} %all-gather.5.cloned.1.call-done, ...), kind=kOutput, calls=%fused_computation.13 | convolution fusion | flops 1240988160 | bytes 40707072 | tf_op jit(solution)/shard_map/sghd,kgd->ghsk/dot_general | solution.py:27
  135.1 9.1 %fusion.21 = bf16[6144,128]{0,1:T(8,128)(2,1)S(1)} fusion(f32[6144,192,4]{0,1,2:T(8,128)} %get-tuple-element.20, f32[4,192]{1,0:T(4,128)S(1)} %get-tuple-element.17, pred[192,6144]{1,0:T(8,128)(4,1)S(1)} %fusion.25, bf16[24,4,8,128]{3,2,1,0:T(8,128)(2,1)S(1)} %fusion.38), kind=kOutput, calls=%fused_computation.22 | convolution fusion | flops 1227620352 | bytes 21826560 | tf_op jit(solution)/shard_map/ghsk,sghd->kgd/dot_general | solution.py:90
  144.2 1.6 copy.36
  145.8 0.0 reduce-scatter.7.cloned.1.call-update
  145.8 0.2 reduce-scatter.5.cloned.1.call-start
  146.1 13.7 %fusion.10 = bf16[4,192,6144]{2,1,0:T(8,128)(2,1)S(1)} fusion(f32[192,4,6144]{2,0,1:T(8,128)} %get-tuple-element.21, f32[6144,192,4]{0,1,2:T(8,128)} %get-tuple-element.20, f32[4,192]{1,0:T(4,128)S(1)} %get-tuple-element.18, f32[4,192]{1,0:T(4,128)S(1)} %get-tuple-element.17, pred[192,6144]{1,0:T(8,128)(4,1)S(1)} %fusion.25), kind=kLoop, calls=%fused_computation.15 | loop fusion | flops 33030144 | bytes 48371712 | tf_op jit(solution)/shard_map/reshape.24
  159.8 0.0 copy-start.1
  159.8 3.6 %copy-done.1 = bf16[4,192,6144]{2,1,0:T(8,128)(2,1)} copy-done((bf16[4,192,6144]{2,1,0:T(8,128)(2,1)}, bf16[4,192,6144]{2,1,0:T(8,128)(2,1)S(1)}, u32[]{:S(2)}) %copy-start.1) | copy-done | bytes 9437208
  163.4 0.0 copy-start.2
  163.4 3.9 %fusion.24 = bf16[6144,1,128]{2,0,1:T(8,128)(2,1)} fusion(bf16[4,192,6144]{2,1,0:T(8,128)(2,1)S(1)} %fusion.10, bf16[192,512]{1,0:T(8,128)(2,1)S(1)} %copy-done), kind=kOutput, calls=%fused_computation.23 | convolution fusion | flops 1208745984 | bytes 11206656 | tf_op jit(solution)/shard_map/ghsk,sghd->kgd/dot_general | solution.py:87
  167.3 0.0 reduce-scatter.5.cloned.1.call-update
  167.3 0.0 copy-done.2
  167.3 6.4 %fusion.35 = bf16[192,1,4,128]{3,0,2,1:T(8,128)(2,1)S(1)} fusion(bf16[4,192,6144]{2,1,0:T(8,128)(2,1)} %copy-done.1, bf16[6144,128]{1,0:T(8,128)(2,1)S(1)} %copy-done.2), kind=kOutput, calls=%fused_computation.34 | convolution fusion | flops 1208057856 | bytes 11206656 | tf_op jit(solution)/shard_map/ghsk,kgd->sghd/dot_general | solution.py:86
  173.7 0.2 copy.30
  173.9 0.7 copy.63
  174.6 58.8 %reduce-scatter.7.cloned.1.call-done = bf16[192,128]{1,0:T(8,128)(2,1)} async-done(((bf16[6144,128]{1,0:T(8,128)(2,1)}), bf16[192,128]{1,0:T(8,128)(2,1)}) %reduce-scatter.7.cloned.1.call-update) | async-done | bytes 49168
  233.4 92.1 %reduce-scatter.5.cloned.1.call-done = bf16[192,1,128]{2,0,1:T(8,128)(2,1)} async-done(((bf16[6144,1,128]{2,0,1:T(8,128)(2,1)}), bf16[192,1,128]{2,0,1:T(8,128)(2,1)}) %reduce-scatter.5.cloned.1.call-update) | async-done | bytes 49168 | tf_op jit(solution)/shard_map/reduce_scatter | solution.py:97
  (3 shorter events, 0.0 us)
Async XLA Ops:
  7.2 59.6 %copy-start = (bf16[192,512]{1,0:T(8,128)(2,1)S(1)}, bf16[192,512]{1,0:T(8,128)(2,1)}, u32[]{:S(2)}) copy-start(bf16[192,512]{1,0:T(8,128)(2,1)} %param.6) | copy-start | bytes 589828
  7.2 59.5 %all-gather.3.cloned.1.call-start = ((), (), s32[]{:S(2)}) async-start(), calls=%async_computation.3 | async-start | bytes 1622016 | tf_op jit(solution)/shard_map/all_gather | solution.py:76
  10.1 26.2 %all-to-all-start = ((bf16[8,192,512]{2,1,0:T(8,128)(2,1)}), bf16[8,192,512]{2,1,0:T(8,128)(2,1)S(1)}, u32[]{:S(2)}, u32[]{:S(2)}) async-start(bf16[8,192,512]{2,1,0:T(8,128)(2,1)} %stack.2), calls=%async_computation | async-start | bytes 3145728 | tf_op jit(solution)/shard_map/all_to_all | solution.py:45
  16.4 103.2 %all-gather.5.cloned.1.call-start = ((), (), s32[]{:S(2)}) async-start(), calls=%async_computation.4 | async-start | bytes 1622016 | tf_op jit(solution)/shard_map/all_gather | solution.py:77
  17.1 216.2 %reduce-scatter.7.cloned.1.call-start = ((), (), s32[]{:S(2)}) async-start(), calls=%async_computation.6 | async-start | bytes 1622016
  145.8 179.7 %reduce-scatter.5.cloned.1.call-start = ((), (), s32[]{:S(2)}) async-start(), calls=%async_computation.5 | async-start | bytes 1622016 | tf_op jit(solution)/shard_map/reduce_scatter | solution.py:97
  159.8 3.6 %copy-start.1 = (bf16[4,192,6144]{2,1,0:T(8,128)(2,1)}, bf16[4,192,6144]{2,1,0:T(8,128)(2,1)S(1)}, u32[]{:S(2)}) copy-start(bf16[4,192,6144]{2,1,0:T(8,128)(2,1)S(1)} %fusion.10) | copy-start | bytes 28311556
  163.4 3.9 %copy-start.2 = (bf16[6144,128]{1,0:T(8,128)(2,1)S(1)}, bf16[6144,128]{1,0:T(8,128)(2,1)}, u32[]{:S(2)}) copy-start(bf16[6144,128]{1,0:T(8,128)(2,1)} %all-gather.3.cloned.1.call-done) | copy-start | bytes 4718596
Sparse Core Ops, SparseCore 0:
  10.6 56.1 all-gather.2
  69.3 50.2 all-gather.4
  146.0 87.3 reduce-scatter.6
  237.6 87.8 reduce-scatter.4
